TPU v7x, 128 devices: a whole 4x4x4 slice. The times are simulated.
128 devices in a mesh: gx: 8 (over x, core), gy: 16 (over z, y).
Axes of the slice: x: 4, y: 4, z: 4, core: 2. Of those that a mesh axis runs over, the one named last changes fastest.
Arguments:
- positions: float32 [3, 16, 32, 8, 128], P(None, 'gx', 'gy'), may hold values from 0 to 1, as said below
- velocities: float32 [3, 16, 32, 8, 128], P(None, 'gx', 'gy'), may hold values from -6 to 6
- kicks: float32 [3, 16, 32, 8, 128], P(None, 'gx', 'gy'), may hold values from -6 to 6
- counts: int32 [16, 32, 8], P('gx', 'gy'), may hold values from 64 to 128, as said below
- subcell: int32 [16, 32, 8, 128], P('gx', 'gy'), may hold values from 0 to 26, as said below
- electron_temp: float32 [48, 96, 24], P('gx', 'gy'), may hold values from 1 to 2
- laser_flux: float32 [48, 96], P('gx', 'gy'), may hold values from 1 to 10
Outputs:
- next_velocities: float32 [3, 16, 32, 8, 128], P(None, 'gx', 'gy')
- next_temperature: float32 [48, 96, 24], P('gx', 'gy')
Inputs may be any that keep to these rules, and one draw needn't show every extreme that they name: `counts`: at least one tile holds exactly 128 live atoms. subcell = 9 a + 3 b + c for the atom's grid cell offsets a, b, c along x, y, z within its tile. `positions`: each component lies in the grid cell named by subcell: component x in [a/3, (a+1)/3), likewise y with b and z with c.
All inputs are finite; a program needn't handle non-finite values.
Results may differ from a plain program's by a relative error of at most 0.0003.
Values sent between devices are 32-bit elements; how exact they have to be, the bound alone decides.
A program may use at most 128 MiB of HBM per device.

v0:
```python
import jax
import jax.numpy as jnp
import numpy as np
from jax import lax
from jax.experimental import pallas as pl
from jax.experimental.pallas import tpu as pltpu
from jax.sharding import PartitionSpec as P

ROOT = float(np.sqrt(5.0))
FAR = 1000.0 * ROOT
ROWS = 4096 + 64
TILES = 32
RANK_KEY = 1024
FAST = 3
f32 = jnp.float32
SIDES = [(dx, dy) for dx in (-1, 0, 1) for dy in (-1, 0, 1) if (dx, dy) != (0, 0)]


COLUMN = 24
BLOCKS = 384
CHUNK = 32
STEP = 4
SPARE = 4128


def where_of(n):
    col, o, z = n // 64, n // 8 % 8, n % 8
    ox, oy, oz = o // 4, o // 2 % 2, o % 2
    return col, o, z, ((col // 2 + ox) * 3 + (col % 2 + oy)) * 9 + z + oz


def static_tables():
    col, o, z, vertex = (np.array(k) for k in zip(*(where_of(n) for n in range(256))))
    order = np.argsort(vertex, kind="stable")
    rank = np.zeros(256, np.int64)
    rank[order] = np.arange(256)
    before = rank[:, None] < rank[None, :]
    tile = col * 8 + z
    inside = (tile[:, None] == tile[None, :]) & (o[:, None] < o[None, :])
    at = vertex[:, None] == np.arange(128)[None, :]
    start = np.arange(128)[:, None] > vertex[None, :]
    return order.astype(np.int32), before, inside, at, start


def span(d, sender):
    if d == 0:
        return slice(0, 2) if sender else slice(1, 3)
    if sender:
        return slice(1, 2) if d > 0 else slice(0, 1)
    return slice(0, 1) if d > 0 else slice(3, 4)


def neighbour(dx, dy):
    nx, ny = lax.axis_size("gx"), lax.axis_size("gy")
    return (
        lax.rem(lax.axis_index("gx") + dx + nx, nx),
        lax.rem(lax.axis_index("gy") + dy + ny, ny),
    )


def greet():
    barrier = pltpu.get_barrier_semaphore()
    for dx, dy in SIDES:
        pl.semaphore_signal(
            barrier, inc=1, device_id=neighbour(dx, dy), device_id_type=pl.DeviceIdType.MESH
        )
    pl.semaphore_wait(barrier, len(SIDES))


def remote(src, dst, send, recv, dx, dy):
    return pltpu.make_async_remote_copy(
        src_ref=src,
        dst_ref=dst,
        send_sem=send,
        recv_sem=recv,
        device_id=neighbour(dx, dy),
        device_id_type=pl.DeviceIdType.MESH,
    )


def iota(shape, dim):
    return lax.broadcasted_iota(jnp.int32, shape, dim)


def wide(column):
    return jnp.broadcast_to(column, (8, 128))


def gather_kernel(
    pos_h, vel_h, kick_h, cnt_h, sub_h, te_h, flux_h, upper_h, before_h, inside_h, at_h, start_h,
    jf_h, key_h, tab_h, heat_h, pv_h, rows_h,
    pos, vel, kick, cnt, sub, te, flux, upper, before, inside, at, start,
    jf, key, tab, heat, pv, rows,
    halo, cbuf, hot, order, feat, insem, outsem, ssem, rsem, csem, dsem,
):
    loads = [
        pltpu.make_async_copy(src, dst, insem.at[n])
        for n, (src, dst) in enumerate(
            zip(
                (cnt_h, pos_h, upper_h, sub_h, te_h, vel_h, kick_h, flux_h, before_h, inside_h, at_h, start_h),
                (cnt, pos, upper, sub, te, vel, kick, flux, before, inside, at, start),
                strict=True,
            )
        )
    ]
    for c in loads:
        c.start()
    greet()
    copies = []
    for n, (dx, dy) in enumerate(SIDES):
        copies.append(
            remote(
                pos_h.at[:, span(dx, True), span(dy, True)],
                halo.at[:, span(dx, False), span(dy, False)],
                ssem.at[n], rsem.at[n], dx, dy,
            )
        )
        copies.append(remote(cnt_h, cbuf.at[n], csem.at[n], dsem.at[n], dx, dy))
    for c in copies:
        c.start()
    stores = [
        pltpu.make_async_copy(src, dst, outsem.at[n])
        for n, (src, dst) in enumerate(
            zip((rows, pv, heat, key, tab, jf), (rows_h, pv_h, heat_h, key_h, tab_h, jf_h), strict=True)
        )
    ]

    lane, row = iota((8, 128), 1), iota((8, 128), 0)
    pick = iota((8, 8), 0) == iota((8, 8), 1)
    deep = row.astype(f32) - 4.0

    def alive(counts):
        column = jnp.sum(jnp.where(pick, counts.astype(f32), 0.0), axis=1, keepdims=True)
        return lane < wide(column).astype(jnp.int32)

    def features(hx, hy, xyz, live):
        first = (hx * 4 + hy) * COLUMN + 8
        out = []
        for n, off in enumerate((float(hx - 2), float(hy - 2), deep)):
            out.append(jnp.where(live, (xyz[n] + off) * ROOT, FAR))
            jf[n, first : first + 8, :] = out[n]
        jf[3, first : first + 8, :] = -(out[0] * out[0] + out[1] * out[1] + out[2] * out[2])
        return out

    for col in range(16):
        for n in range(4):
            empty = jnp.full((8, 128), FAR if n < 3 else -3.0 * FAR * FAR, f32)
            jf[n, col * COLUMN : col * COLUMN + 8, :] = empty
            jf[n, col * COLUMN + 16 : col * COLUMN + 24, :] = empty

    for c in loads[:3]:
        c.wait()
    place = iota((128, 128), 0)
    ones = jnp.ones((128, 128), jnp.bfloat16)
    for n in range(9, 16):
        feat[:, n, :] = jnp.zeros((8, 128), f32)
    for col in range(4):
        tx, ty = col // 2, col % 2
        live = alive(cnt[tx, pl.ds(ty, 8, stride=0), :])
        xyz = [pos[n, tx, ty] for n in range(3)]
        own = features(tx + 1, ty + 1, xyz, live)
        octant = sum(
            jnp.where(xyz[n] >= 0.5, s, 0) for n, s in enumerate((4, 2, 1))
        )
        octant = jnp.where(live, octant, -1)
        for o in range(8):
            hot[col * 64 + o * 8 : col * 64 + o * 8 + 8, :] = jnp.where(octant == o, 1.0, 0.0)
        mine = hot[col * 64 : col * 64 + 64, :].astype(jnp.bfloat16)
        upto = jnp.dot(mine, upper[...], preferred_element_type=f32)
        total = jnp.dot(mine, ones, preferred_element_type=f32)
        rank = jnp.zeros((8, 128), f32)
        slot = jnp.zeros((8, 128), f32)
        ahead = jnp.zeros((8, 128), f32)
        for o in range(8):
            here = upto[o * 8 : o * 8 + 8, :]
            rank = jnp.where(octant == o, here, rank)
            slot = jnp.where(octant == o, here + ahead, slot)
            ahead = ahead + total[o * 8 : o * 8 + 8, :]
        key[col * 8 : col * 8 + 8, :] = jnp.where(
            live, octant * RANK_KEY + rank.astype(jnp.int32) - 1, -1
        )
        order[col * 8 : col * 8 + 8, :] = jnp.where(live, slot.astype(jnp.int32) - 1, -1)
        for n in range(3):
            high = own[n].astype(jnp.bfloat16).astype(f32)
            rest = own[n] - high
            middle = rest.astype(jnp.bfloat16).astype(f32)
            feat[:, n, :] = high
            feat[:, 3 + n, :] = middle
            feat[:, 6 + n, :] = rest - middle
        for z in range(8):
            tile = col * 8 + z
            hit = order[pl.ds(tile, 128, stride=0), :] == place
            rows[tile * 128 : tile * 128 + 128, 0:16] = lax.dot_general(
                jnp.where(hit, 1.0, 0.0).astype(jnp.bfloat16),
                feat[z].astype(jnp.bfloat16),
                (((1,), (1,)), ((), ())),
                preferred_element_type=f32,
            )
    stores[0].start()

    for c in loads[3:8]:
        c.wait()
    for col in range(4):
        tx, ty = col // 2, col % 2
        live = alive(cnt[tx, pl.ds(ty, 8, stride=0), :])
        cell = jnp.where(live, sub[tx, ty], -1)
        te_atom = jnp.zeros((8, 128), f32)
        for a in range(3):
            for b in range(3):
                line = te[tx * 3 + a, pl.ds(ty * 3 + b, 8, stride=0), :]
                for c in range(3):
                    third = iota((8, 24), 1) == 3 * iota((8, 24), 0) + c
                    value = jnp.sum(jnp.where(third, line, 0.0), axis=1, keepdims=True)
                    te_atom = jnp.where(cell == 9 * a + 3 * b + c, wide(value), te_atom)
        sigma = jnp.sqrt(0.2 * te_atom)
        v = [vel[n, tx, ty] for n in range(3)]
        k = [kick[n, tx, ty] for n in range(3)]
        for n in range(3):
            pv[n, col * 8 : col * 8 + 8, :] = jnp.where(live, 0.9 * v[n] + sigma * k[n], 0.0)
        work = 0.1 * (v[0] * v[0] + v[1] * v[1] + v[2] * v[2]) - sigma * (
            k[0] * v[0] + k[1] * v[1] + k[2] * v[2]
        )
        depth = jnp.exp((iota((1, 128), 1).astype(f32) + 0.5) * (-1.0 / 38.0)) * 0.05
        for a in range(3):
            for b in range(3):
                grid = jnp.zeros((8, 128), f32)
                for c in range(3):
                    part = jnp.where(cell == 9 * a + 3 * b + c, work, 0.0)
                    value = wide(jnp.sum(part, axis=1, keepdims=True))
                    grid = jnp.where(lane == 3 * row + c, value, grid)
                gained = jnp.sum(grid, axis=0, keepdims=True)
                base = te[tx * 3 + a, ty * 3 + b : ty * 3 + b + 1, :]
                light = flux[tx * 3 + a, ty * 3 + b] * depth
                heat[tx, ty, a, b : b + 1, :] = gained * (1.0 / 40.0) + light
                heat[tx, ty, a, b : b + 1, 0:24] = heat[tx, ty, a, b : b + 1, 0:24] + base
        for a in range(3):
            heat[tx, ty, a, 3:8, :] = jnp.zeros((5, 128), f32)
    for c in stores[1:4]:
        c.start()

    for c in loads[8:]:
        c.wait()
    bf = jnp.bfloat16
    both = (((1,), (1,)), ((), ()))
    count = lax.dot_general(ones[0:8], hot[...].astype(bf), both, preferred_element_type=f32)
    few = count.astype(bf)
    base = jnp.dot(few, before[...], preferred_element_type=f32)
    skip = jnp.dot(few, inside[...], preferred_element_type=f32)
    item = iota((1, 256), 1)
    tile = lax.shift_right_logical(item, 6) * 8 + (item & 7)
    tab[...] = jnp.zeros((8, BLOCKS), jnp.int32)
    tab[0:1, 0:256] = base[0:1, :].astype(jnp.int32)
    tab[1:2, 0:256] = skip[0:1, :].astype(jnp.int32) + tile * 128
    tab[2:3, 0:256] = count[0:1, :].astype(jnp.int32)
    many = jnp.dot(few, at[...], preferred_element_type=f32)
    blocks = lax.shift_right_logical(many.astype(jnp.int32) + 15, 4).astype(f32)
    rep = jnp.broadcast_to(blocks[0:1, :], (128, 128)).astype(bf)
    under = jnp.where(iota((128, 128), 1) < place, 1.0, 0.0).astype(bf)
    upon = jnp.where(iota((128, 128), 1) <= place, 1.0, 0.0).astype(bf)
    low_block = lax.dot_general(under, rep, both, preferred_element_type=f32)
    top_block = lax.dot_general(upon, rep, both, preferred_element_type=f32)
    first = lax.dot_general(
        start[...], jnp.broadcast_to(few[0:1, :].astype(f32), (128, 256)).astype(bf), both, preferred_element_type=f32
    )
    for j in range(BLOCKS // 128):
        b = (lane + 128 * j).astype(f32)
        begin = jnp.zeros((8, 128), f32)
        low = jnp.zeros((8, 128), f32)
        for r in range(11):
            base_tile = jnp.zeros((8, 128), f32)
            for s in range(8):
                v = r * 8 + s
                if v < 81:
                    c = v // 9
                    base_tile = jnp.where(
                        row == s, float(((c // 3) * 4 + c % 3) * COLUMN + 7 + v % 9), base_tile
                    )
            lo = low_block[r * 8 : r * 8 + 8, :]
            hit = (lo <= b) & (b < top_block[r * 8 : r * 8 + 8, :])
            begin = begin + jnp.where(hit, first[r * 8 : r * 8 + 8, :] + 16.0 * (b - lo) - SPARE, 0.0)
            low = low + jnp.where(hit, base_tile, 0.0)
        tab[3:4, j * 128 : j * 128 + 128] = (jnp.sum(begin, axis=0, keepdims=True) + SPARE).astype(jnp.int32)
        tab[4:5, j * 128 : j * 128 + 128] = jnp.sum(low, axis=0, keepdims=True).astype(jnp.int32)
    tab[5:6, 0:128] = top_block[127:128, :].astype(jnp.int32)
    stores[4].start()

    for c in copies:
        c.wait()
    for n, (dx, dy) in enumerate(SIDES):
        for hx in range(4)[span(dx, False)]:
            for hy in range(4)[span(dy, False)]:
                sx = hx - 1 if dx == 0 else (1 if dx > 0 else 0)
                sy = hy - 1 if dy == 0 else (1 if dy > 0 else 0)
                live = alive(cbuf[n, sx, pl.ds(sy, 8, stride=0), :])
                features(hx, hy, [halo[m, hx, hy] for m in range(3)], live)
    stores[5].start()
    for c in stores:
        c.wait()


def exchange_kernel(t, heat, t_all, heat_all, own, ssem, rsem, csem, dsem):
    mine = [
        pltpu.make_async_copy(t, t_all.at[1:3, 1:3], own.at[0]),
        pltpu.make_async_copy(heat, heat_all.at[1:3, 1:3], own.at[1]),
    ]
    for c in mine:
        c.start()
    greet()
    copies = []
    for n, (dx, dy) in enumerate(SIDES):
        sx, sy, rx, ry = span(dx, True), span(dy, True), span(dx, False), span(dy, False)
        copies.append(remote(t.at[sx, sy], t_all.at[rx, ry], ssem.at[n], rsem.at[n], dx, dy))
        copies.append(remote(heat.at[sx, sy], heat_all.at[rx, ry], csem.at[n], dsem.at[n], dx, dy))
    for c in copies:
        c.start()
    for c in mine + copies:
        c.wait()


def own_tile(tile):
    return (tile // 16 + 1) * (4 * COLUMN) + (tile // 8 % 2 + 1) * COLUMN + tile % 8 + 8


def pack_rows(tab, order, rows, packed):
    def step(i, carry):
        items = [order[i * 8 + u] for u in range(8)]
        widest = tab[2, items[0]]
        for item in items[1:]:
            widest = jnp.maximum(widest, tab[2, item])

        @pl.when(widest <= FAST * 8)
        def _():
            for item in items:
                src, dst = tab[1, item], tab[0, item]
                for k in range(FAST):
                    packed[pl.ds(dst + 8 * k, 8), :] = rows[pl.ds(src + 8 * k, 8), :]

        @pl.when(widest > FAST * 8)
        def _():
            def one(u, carry):
                item = order[i * 8 + u]
                src, dst = tab[1, item], tab[0, item]

                def inner(k, carry):
                    packed[pl.ds(dst + 8 * k, 8), :] = rows[pl.ds(src + 8 * k, 8), :]
                    return carry

                return lax.fori_loop(0, (tab[2, item] + 7) // 8, inner, carry)

            lax.fori_loop(0, 8, one, 0)

        return carry

    lax.fori_loop(0, 32, step, 0)


def over_tiles(tab, chunk, put, zero):
    def step(tile, carry):
        first = tile // 8 * 64 + tile % 8
        widest = tab[2, first]
        for o in range(1, 8):
            widest = jnp.maximum(widest, tab[2, first + o * 8])

        @pl.when(widest <= FAST * 8)
        def _():
            lanes = zero
            for o in range(8):
                for k in range(FAST):
                    lanes = chunk(first + o * 8, tile, o, k, lanes)
            put(tile, lanes)

        @pl.when(widest > FAST * 8)
        def _():
            def per(o, lanes):
                item = first + o * 8

                def inner(k, lanes):
                    return chunk(item, tile, o, k, lanes)

                return lax.fori_loop(0, (tab[2, item] + 7) // 8, inner, lanes)

            put(tile, lax.fori_loop(0, 8, per, zero))

        return carry

    lax.fori_loop(0, TILES, step, 0)


def around(low):
    return [low + (dx * 4 + dy) * COLUMN + dz for dx in (0, 1) for dy in (0, 1) for dz in (0, 1)]


def matcher(key):
    sub = iota((8, 128), 0)

    def match(tile, octant, k):
        return key[pl.ds(tile, 8, stride=0), :] == sub + (octant * RANK_KEY + k * 8)

    return match


def slope_of(tot):
    return wide(0.1875 + 0.625 * lax.rsqrt(jnp.sum(tot, axis=1, keepdims=True)))


def density_kernel(
    tab_h, order_h, jf_h, key_h, rows_h, w_h, ti_h, tl_h,
    tab, order, jf, key, rows, packed, ti, tl, wb, own, last, insem, outsem, wsem,
):
    loads = [
        pltpu.make_async_copy(src, dst, insem.at[n])
        for n, (src, dst) in enumerate(((tab_h, tab), (order_h, order), (rows_h, rows.at[0:4096]), (jf_h, jf), (key_h, key)))
    ]
    for c in loads:
        c.start()
    for c in loads[:3]:
        c.wait()
    pack_rows(tab, order, rows, packed)
    for c in loads[3:]:
        c.wait()
    count = tab[5, 0]
    third = lax.rem(iota((8, 128), 1), 3)
    masks = [(third == n) & (iota((8, 128), 1) < 9) for n in range(3)]

    def own_rows(b):
        row = tab[3, b]
        out = []
        for k in range(2):
            value = packed[pl.ds(row + 8 * k, 8), :]
            x, y, z = (wide(jnp.sum(jnp.where(m, value, 0.0), axis=1, keepdims=True)) for m in masks)
            out += [x + x, y + y, z + z, 1.0 - (x * x + y * y + z * z)]
        return out

    def keep(blocks):
        for u, values in enumerate(blocks):
            for n, value in enumerate(values):
                own[u, n] = value

    def settle(i, tots):
        for u in range(STEP):
            row = tab[3, i * STEP + u]
            for k in range(2):
                ti[pl.ds(row + 8 * k, 8), :] = slope_of(tots[u][k])

    def step(i, carry):
        tots = [[last[u, k] for k in range(2)] for u in range(STEP)]
        ahead = [own_rows((i + 1) * STEP + u) for u in range(STEP)]
        new = []
        for u in range(STEP):
            b = i * STEP + u
            mine = [[own[u, 4 * k + n] for n in range(4)] for k in range(2)]
            tot = [None, None]
            for n, tile in enumerate(around(tab[4, b])):
                xj, yj, zj, bj = (jf[m, pl.ds(tile, 8, stride=0), :] for m in range(4))
                for k in range(2):
                    x, y, z, a = mine[k]
                    w = jnp.maximum((a + bj) + (x * xj + y * yj + z * zj), 0.0)
                    wb[b, (n * 2 + k) * 8 : (n * 2 + k) * 8 + 8, :] = w
                    cube = w * w * w
                    tot[k] = cube if tot[k] is None else tot[k] + cube
            new.append(tot)
        settle(jnp.maximum(i - 1, 0), tots)
        keep(ahead)
        for u in range(STEP):
            for k in range(2):
                last[u, k] = new[u][k]
        return carry

    def saved(g):
        part = pl.ds(g * CHUNK, CHUNK)
        return pltpu.make_async_copy(wb.at[part], w_h.at[part], wsem.at[g])

    steps = (count + STEP - 1) // STEP
    groups = (count + CHUNK - 1) // CHUNK
    per = CHUNK // STEP

    def group(g, carry):
        lax.fori_loop(g * per, jnp.minimum(g * per + per, steps), step, 0)
        saved(g).start()
        return carry

    keep([own_rows(u) for u in range(STEP)])
    last[...] = jnp.ones_like(last)
    lax.fori_loop(0, groups, group, 0)
    settle(steps - 1, [[last[u, k] for k in range(2)] for u in range(STEP)])
    rows_out = pltpu.make_async_copy(ti, ti_h, outsem.at[0])
    rows_out.start()

    match = matcher(key)

    def finish(item, tile, octant, k, lanes):
        t = ti[pl.ds(tab[0, item] + k * 8, 8), :]
        return lanes + jnp.where(match(tile, octant, k), t, 0.0)

    def put(tile, lanes):
        tl[pl.ds(tile, 1), :] = jnp.sum(lanes, axis=0, keepdims=True)

    over_tiles(tab, finish, put, jnp.zeros((8, 128), f32))
    lanes_out = pltpu.make_async_copy(tl, tl_h, outsem.at[1])
    lanes_out.start()

    def drain(g, carry):
        saved(g).wait()
        return carry

    lax.fori_loop(0, groups, drain, 0)
    rows_out.wait()
    lanes_out.wait()


def diffuse(heat, out, old, new):
    for x in range(12):
        for y in range(4):
            old[x, y * 3 : y * 3 + 8, :] = heat[x // 3, y, x % 3]
    lane = iota((8, 128), 1)
    for s in range(3):
        for x in range(s + 1, 11 - s):
            for r in (1, 9) if s == 0 else (s + 1,):
                t = old[x, r : r + 8, :]
                near = [old[x - 1, r : r + 8, :], old[x + 1, r : r + 8, :], old[x, r - 1 : r + 7, :], old[x, r + 1 : r + 9, :]]
                q = t * t
                side = near[0] * near[0] + near[1] * near[1] + near[2] * near[2] + near[3] * near[3] - 4.0 * q
                up = jnp.where(lane < 23, pltpu.roll(q, 127, 1) - q, 0.0)
                t = t + 0.025 * (side + (up - pltpu.roll(up, 1, 1)))
                if s < 2:
                    new[x, r : r + 8, :] = t
                else:
                    out[x - 3, :, :] = t[0:6, 0:24]
        old, new = new, old


def force_kernel(
    tab_h, w_h, jf_h, tj_h, key_h, ti_h, pv_h, heat_h, vel_h, temp,
    tab, wb, jf, tj, key, ti, pv, heat, vel, fg, fx, fy, fz, last, old, new, insem, outsem, wsem,
):
    def loaded(g):
        part = pl.ds(g * CHUNK, CHUNK)
        return pltpu.make_async_copy(w_h.at[part], wb.at[part], wsem.at[g])

    loads = [
        pltpu.make_async_copy(src, dst, insem.at[n])
        for n, (src, dst) in enumerate(
            (
                (tab_h, tab), (heat_h, heat), (tj_h, tj.at[:, 8:16]), (ti_h, ti),
                (jf_h.at[0:3], jf), (key_h, key), (pv_h, pv),
            )
        )
    ]
    loads[0].start()
    loaded(0).start()
    for c in loads[1:]:
        c.start()
    loads[0].wait()
    count = tab[5, 0]
    groups = (count + CHUNK - 1) // CHUNK

    def fetch(g, carry):
        loaded(g).start()
        return carry

    lax.fori_loop(1, groups, fetch, 0)
    none = jnp.zeros((8, 128), f32)
    for col in range(16):
        tj[col, 0:8, :] = none
        tj[col, 16:24, :] = none
    loads[1].wait()
    diffuse(heat, temp, old, new)
    for c in loads[2:]:
        c.wait()
    sums = (fg, fx, fy, fz)

    def settle(i):
        for u in range(STEP):
            row = tab[3, i * STEP + u]
            for k in range(2):
                for n, f in enumerate(sums):
                    f[pl.ds(row + 8 * k, 8), :] = wide(jnp.sum(last[u, 4 * k + n], axis=1, keepdims=True))

    def step(i, carry):
        settle(jnp.maximum(i - 1, 0))
        new = []
        for u in range(STEP):
            b = i * STEP + u
            low = tab[4, b]
            row = tab[3, b]
            t_own = [ti[pl.ds(row + 8 * k, 8), :] for k in range(2)]
            tot = [None] * 8
            for n, tile in enumerate(around(low)):
                other = [jf[m, pl.ds(tile, 8, stride=0), :] for m in range(3)]
                t_other = tj.at[...].reshape(16 * COLUMN, 128)[pl.ds(tile, 8, stride=0), :]
                for k in range(2):
                    w = wb[b, (n * 2 + k) * 8 : (n * 2 + k) * 8 + 8, :]
                    g = (w * w) * ((t_own[k] + t_other) - w)
                    for m, p in enumerate((g, g * other[0], g * other[1], g * other[2])):
                        at = 4 * k + m
                        tot[at] = p if tot[at] is None else tot[at] + p
            new.append(tot)
        for u in range(STEP):
            for n in range(8):
                last[u, n] = new[u][n]
        return carry

    steps = (count + STEP - 1) // STEP
    per = CHUNK // STEP

    def group(g, carry):
        loaded(g).wait()
        return lax.fori_loop(g * per, jnp.minimum(g * per + per, steps), step, carry)

    last[...] = jnp.zeros_like(last)
    lax.fori_loop(0, groups, group, 0)
    settle(steps - 1)

    match = matcher(key)

    def finish(item, tile, octant, k, lanes):
        row = tab[0, item] + k * 8
        hit = match(tile, octant, k)
        return tuple(
            part + jnp.where(hit, f[pl.ds(row, 8), :], 0.0)
            for part, f in zip(lanes, sums, strict=True)
        )

    def put(tile, lanes):
        total = [jnp.sum(part, axis=0, keepdims=True) for part in lanes]
        at = own_tile(tile)
        live = key[pl.ds(tile, 1), :] >= 0
        for n in range(3):
            pull = jf[n, pl.ds(at, 1), :] * total[0] - total[n + 1]
            vel[n, pl.ds(tile, 1), :] = jnp.where(live, pv[n, pl.ds(tile, 1), :] + pull * (-2.4 / ROOT), 0.0)

    over_tiles(tab, finish, put, (none,) * 4)
    out = pltpu.make_async_copy(vel, vel_h, outsem.at[0])
    out.start()
    out.wait()


VMEM = pl.BlockSpec(memory_space=pltpu.VMEM)
ANY = pl.BlockSpec(memory_space=pltpu.HBM)
LOCAL = pltpu.CompilerParams(vmem_limit_bytes=67043328)


def shape(*dims, dtype=f32):
    return jax.ShapeDtypeStruct(dims, dtype)


def vmem(like):
    return pltpu.VMEM(like.shape, like.dtype)


def meeting(n):
    return pltpu.CompilerParams(collective_id=n, has_side_effects=True, vmem_limit_bytes=67043328)


def local(positions, velocities, kicks, counts, subcell, electron_temp, laser_flux):
    order, *zeroone = static_tables()
    upper = np.triu(np.ones((128, 128)))
    bf = jnp.bfloat16
    i32 = jnp.int32
    dma = pltpu.SemaphoreType.DMA
    around8 = [dma((8,))] * 4
    tiles = shape(3, 2, 2, 8, 128)
    outs = (
        shape(4, 16 * COLUMN, 128),
        shape(TILES, 128, dtype=i32),
        shape(8, BLOCKS, dtype=i32),
        shape(2, 2, 3, 8, 128),
        shape(3, TILES, 128),
        shape(4096, 128),
    )
    jf, key, tab, heat, pv, rows = pl.pallas_call(
        gather_kernel,
        name="gather",
        out_shape=outs,
        in_specs=[ANY] * 12,
        out_specs=(ANY,) * 6,
        scratch_shapes=[
            *(vmem(tiles),) * 3,
            pltpu.VMEM((2, 2, 8), i32),
            pltpu.VMEM((2, 2, 8, 128), i32),
            pltpu.VMEM((6, 6, 24), f32),
            pltpu.SMEM((6, 6), f32),
            pltpu.VMEM((128, 128), bf),
            *(pltpu.VMEM(m.shape, bf) for m in zeroone),
            *(vmem(o) for o in outs),
            pltpu.VMEM((3, 4, 4, 8, 128), f32),
            pltpu.VMEM((8, 2, 2, 8), i32),
            pltpu.VMEM((256, 128), f32),
            pltpu.VMEM((TILES, 128), i32),
            pltpu.VMEM((8, 16, 128), f32),
            dma((12,)),
            dma((6,)),
            *around8,
        ],
        compiler_params=meeting(0),
    )(
        positions, velocities, kicks, counts, subcell, electron_temp, laser_flux,
        *(jnp.asarray(m, bf) for m in (upper, *zeroone)),
    )
    order = jnp.asarray(order)
    row = shape(ROWS, 128)
    w, ti, tl = pl.pallas_call(
        density_kernel,
        name="density",
        out_shape=(shape(BLOCKS, 128, 128), row, shape(TILES, 128)),
        in_specs=[ANY] * 5,
        out_specs=(ANY,) * 3,
        scratch_shapes=[
            pltpu.SMEM((8, BLOCKS), i32),
            pltpu.SMEM((256,), i32),
            vmem(outs[0]),
            vmem(outs[1]),
            vmem(row),
            vmem(row),
            vmem(row),
            pltpu.VMEM((TILES, 128), f32),
            pltpu.VMEM((BLOCKS, 128, 128), f32),
            pltpu.VMEM((STEP, 8, 8, 128), f32),
            pltpu.VMEM((STEP, 2, 8, 128), f32),
            dma((5,)),
            dma((2,)),
            dma((BLOCKS // CHUNK,)),
        ],
        compiler_params=LOCAL,
    )(tab, order, jf, key, rows)
    t_all, heat = pl.pallas_call(
        exchange_kernel,
        name="exchange",
        out_shape=(shape(4, 4, 8, 128), shape(4, 4, 3, 8, 128)),
        in_specs=[ANY] * 2,
        out_specs=(ANY,) * 2,
        scratch_shapes=[dma((2,)), *around8],
        compiler_params=meeting(1),
    )(tl.reshape(2, 2, 8, 128), heat)
    vel, temp = pl.pallas_call(
        force_kernel,
        name="force",
        out_shape=(shape(3, TILES, 128), shape(6, 6, 24)),
        in_specs=[ANY] * 8,
        out_specs=(ANY, VMEM),
        scratch_shapes=[
            pltpu.SMEM((8, BLOCKS), i32),
            pltpu.VMEM((BLOCKS, 128, 128), f32),
            pltpu.VMEM((3, 16 * COLUMN, 128), f32),
            pltpu.VMEM((16, COLUMN, 128), f32),
            vmem(outs[1]),
            vmem(row),
            vmem(outs[4]),
            pltpu.VMEM((4, 4, 3, 8, 128), f32),
            vmem(outs[4]),
            *(vmem(row),) * 4,
            pltpu.VMEM((STEP, 8, 8, 128), f32),
            *(pltpu.VMEM((12, 24, 128), f32),) * 2,
            dma((7,)),
            dma((1,)),
            dma((BLOCKS // CHUNK,)),
        ],
        compiler_params=LOCAL,
    )(tab, w, jf, t_all.reshape(16, 8, 128), key, ti, pv, heat)
    return (vel.reshape(3, 2, 2, 8, 128), temp)


def solution(mesh):
    in_specs = (
        P(None, "gx", "gy", None, None),
        P(None, "gx", "gy", None, None),
        P(None, "gx", "gy", None, None),
        P("gx", "gy", None),
        P("gx", "gy", None, None),
        P("gx", "gy", None),
        P("gx", "gy"),
    )
    out_specs = (P(None, "gx", "gy", None, None), P("gx", "gy", None))
    return jax.shard_map(local, mesh=mesh, in_specs=in_specs, out_specs=out_specs, check_vma=False)
```

profile of v0, /device:TPU:1, one launch (start us, length us, event | category | flops | bytes accessed | tf_op | source)
XLA Modules:
  0.0 57.4 jit_solution(12287769694540721105)
XLA Ops:
  0.6 13.9 %gather.1 = (f32[4,384,128]{2,1,0:T(8,128)}, s32[32,128]{1,0:T(8,128)}, s32[8,384]{1,0:T(8,128)}, f32[2,2,3,8,128]{4,3,2,1,0:T(8,128)}, f32[3,32,128]{2,1,0:T(8,128)}, /*index=5*/f32[4096,128]{1,0:T(8,128)}) custom-call(f32[3,2,2,8,128]{4,3,2,1,0:T(8,128)} %pos_h.1, f32[3,2,2,8,128]{4,3,2,1,0:T(8,128)} %vel_h.1, f32[3,2,2,8,128]{4,3,2,1,0:T(8,128)} %kick_h.1, ...), custom_call_target="tpu_custom_call" | custom-call | tf_op jit(solution)/shard_map/gather/pallas_call | solution.py:671
  14.5 18.9 %density.1 = (f32[384,128,128]{2,1,0:T(8,128)}, f32[4160,128]{1,0:T(8,128)}, f32[32,128]{1,0:T(8,128)}) custom-call(s32[8,384]{1,0:T(8,128)} %get-tuple-element.15.tab_h, s32[256]{0:T(256)} %constant.17.clone.order_h, f32[4,384,128]{2,1,0:T(8,128)} %get-tuple-element.16.jf_h, s32[32,128]{1,0:T(8,128)} %get-tuple-element.17.key_h, ...), custom_call_target="tpu_custom_call" | custom-call | tf_op jit(solution)/shard_map/density/pallas_call | solution.py:702
  33.5 9.5 %exchange.1 = (f32[4,4,8,128]{3,2,1,0:T(8,128)}, f32[4,4,3,8,128]{4,3,2,1,0:T(8,128)}) custom-call(f32[2,2,8,128]{3,2,1,0:T(8,128)} %bitcast.4, f32[2,2,3,8,128]{4,3,2,1,0:T(8,128)} %get-tuple-element.21.heat), custom_call_target="tpu_custom_call" | custom-call | tf_op jit(solution)/shard_map/exchange/pallas_call | solution.py:726
  43.0 14.4 %force.1 = (f32[3,32,128]{2,1,0:T(8,128)}, f32[6,6,24]{2,1,0:T(8,128)}) custom-call(s32[8,384]{1,0:T(8,128)} %get-tuple-element.15.tab_h, f32[384,128,128]{2,1,0:T(8,128)} %get-tuple-element.19.w_h, f32[4,384,128]{2,1,0:T(8,128)} %get-tuple-element.16.jf_h, f32[16,8,128]{2,1,0:T(8,128)} %bitcast.3, s32[32,128]{1,0:T(8,128)} %get-tuple-element.17.key_h, ...), custom_call_target="tpu_custom_call" | custom-call | tf_op jit(solution)/shard_map/force/pallas_call | solution.py:735
where the time goes:
time: 57.7 us; the launch traced here: 57.4 us
  Pallas kernels  56.7 us (98%)
  between operations  0.66 us (1%)
    pallas_call x1, Pallas kernels, local(): pl.pallas_call(density_kernel, name='density', out_shape=(shape(BLOCKS, 1...  18.9 us
    pallas_call x1, Pallas kernels, local(): pl.pallas_call(force_kernel, name='force', out_shape=(shape(3, TILES, 128...  14.4 us
    pallas_call x1, Pallas kernels, local(): pl.pallas_call(gather_kernel, name='gather', out_shape=outs, in_specs=[AN...  13.9 us
    pallas_call x1, Pallas kernels, local(): pl.pallas_call(exchange_kernel, name='exchange', out_shape=(shape(4, 4, 8...  9.51 us

commit v1 on v0

--- a/solution.py
+++ b/solution.py
@@ -8,19 +8,20 @@
 
 ROOT = float(np.sqrt(5.0))
 FAR = 1000.0 * ROOT
-ROWS = 4096 + 64
 TILES = 32
 RANK_KEY = 1024
 FAST = 3
 f32 = jnp.float32
 SIDES = [(dx, dy) for dx in (-1, 0, 1) for dy in (-1, 0, 1) if (dx, dy) != (0, 0)]
-
-
 COLUMN = 24
-BLOCKS = 384
+PER = 1
+BLOCK = 8 * PER
+BLOCKS = 608 if PER == 1 else 352
+TAB = 640
+ROWS = BLOCKS * BLOCK + 64
 CHUNK = 32
-STEP = 4
-SPARE = 4128
+STEP = 8 // PER
+WIDE = 72 * PER
 
 
 def where_of(n):
@@ -34,12 +35,16 @@
     order = np.argsort(vertex, kind="stable")
     rank = np.zeros(256, np.int64)
     rank[order] = np.arange(256)
-    before = rank[:, None] < rank[None, :]
+    place = (vertex[:, None] == vertex[None, :]) & (rank[:, None] < rank[None, :])
     tile = col * 8 + z
     inside = (tile[:, None] == tile[None, :]) & (o[:, None] < o[None, :])
+    same = np.eye(256, dtype=bool)
+    by_item = np.concatenate([place, place[:, order], inside[:, order], same[:, order]], axis=1)
     at = vertex[:, None] == np.arange(128)[None, :]
-    start = np.arange(128)[:, None] > vertex[None, :]
-    return order.astype(np.int32), before, inside, at, start
+    lower = np.arange(128)[:, None] < vertex[None, :]
+    by_vertex = np.concatenate([lower, lower[:, order]], axis=1)
+    source = (col[order] * 128 * 8 + z[order])[None, :].repeat(8, 0).astype(np.int32)
+    return by_item, at, by_vertex, source
 
 
 def span(d, sender):
@@ -87,9 +92,9 @@
 
 
 def gather_kernel(
-    pos_h, vel_h, kick_h, cnt_h, sub_h, te_h, flux_h, upper_h, before_h, inside_h, at_h, start_h,
+    pos_h, vel_h, kick_h, cnt_h, sub_h, te_h, flux_h, upper_h, by_item_h, at_h, by_vertex_h, source_h,
     jf_h, key_h, tab_h, heat_h, pv_h, rows_h,
-    pos, vel, kick, cnt, sub, te, flux, upper, before, inside, at, start,
+    pos, vel, kick, cnt, sub, te, flux, upper, by_item, at, by_vertex, source,
     jf, key, tab, heat, pv, rows,
     halo, cbuf, hot, order, feat, insem, outsem, ssem, rsem, csem, dsem,
 ):
@@ -97,8 +102,8 @@
         pltpu.make_async_copy(src, dst, insem.at[n])
         for n, (src, dst) in enumerate(
             zip(
-                (cnt_h, pos_h, upper_h, sub_h, te_h, vel_h, kick_h, flux_h, before_h, inside_h, at_h, start_h),
-                (cnt, pos, upper, sub, te, vel, kick, flux, before, inside, at, start),
+                (cnt_h, pos_h, upper_h, sub_h, te_h, vel_h, kick_h, flux_h, by_item_h, at_h, by_vertex_h, source_h),
+                (cnt, pos, upper, sub, te, vel, kick, flux, by_item, at, by_vertex, source),
                 strict=True,
             )
         )
@@ -187,15 +192,17 @@
             feat[:, n, :] = high
             feat[:, 3 + n, :] = middle
             feat[:, 6 + n, :] = rest - middle
+        every = feat[...].reshape(128, 128)
+        block = jnp.zeros((128, 128), f32)
         for z in range(8):
-            tile = col * 8 + z
-            hit = order[pl.ds(tile, 128, stride=0), :] == place
-            rows[tile * 128 : tile * 128 + 128, 0:16] = lax.dot_general(
+            hit = order[pl.ds(col * 8 + z, 128, stride=0), :] == place
+            block = block + lax.dot_general(
                 jnp.where(hit, 1.0, 0.0).astype(jnp.bfloat16),
-                feat[z].astype(jnp.bfloat16),
+                jnp.where(lax.shift_right_logical(place, 4) == z, every, 0.0).astype(jnp.bfloat16),
                 (((1,), (1,)), ((), ())),
                 preferred_element_type=f32,
             )
+        rows[col * 128 : col * 128 + 128, :] = block
     stores[0].start()
 
     for c in loads[3:8]:
@@ -244,44 +251,53 @@
     both = (((1,), (1,)), ((), ()))
     count = lax.dot_general(ones[0:8], hot[...].astype(bf), both, preferred_element_type=f32)
     few = count.astype(bf)
-    base = jnp.dot(few, before[...], preferred_element_type=f32)
-    skip = jnp.dot(few, inside[...], preferred_element_type=f32)
-    item = iota((1, 256), 1)
-    tile = lax.shift_right_logical(item, 6) * 8 + (item & 7)
-    tab[...] = jnp.zeros((8, BLOCKS), jnp.int32)
-    tab[0:1, 0:256] = base[0:1, :].astype(jnp.int32)
-    tab[1:2, 0:256] = skip[0:1, :].astype(jnp.int32) + tile * 128
-    tab[2:3, 0:256] = count[0:1, :].astype(jnp.int32)
+    sums = jnp.dot(few, by_item[...], preferred_element_type=f32).astype(jnp.int32)
     many = jnp.dot(few, at[...], preferred_element_type=f32)
-    blocks = lax.shift_right_logical(many.astype(jnp.int32) + 15, 4).astype(f32)
+    blocks = lax.shift_right_logical(many.astype(jnp.int32) + (BLOCK - 1), 3 if PER == 1 else 4)
+    blocks = blocks.astype(f32)
+    begin = jnp.dot(blocks.astype(bf), by_vertex[...], preferred_element_type=f32).astype(jnp.int32) * BLOCK
+    number = count.astype(jnp.int32)
+    lined = sums[:, 768:1024]
+
+    def widest(values, shifts):
+        for s in shifts:
+            values = jnp.maximum(values, pltpu.roll(values, 256 - s, 1))
+        return values
+
+    table = (
+        sums[:, 0:256] + begin[:, 0:256],
+        number,
+        widest(number, (8, 16, 32)),
+        sums[:, 512:768] * 8 + source[...],
+        sums[:, 256:512] + begin[:, 256:512],
+        lined,
+        widest(lined, (1, 2, 4)),
+    )
+    for n, values in enumerate(table):
+        tab[n : n + 1, 0:256] = values[0:1, :]
     rep = jnp.broadcast_to(blocks[0:1, :], (128, 128)).astype(bf)
     under = jnp.where(iota((128, 128), 1) < place, 1.0, 0.0).astype(bf)
     upon = jnp.where(iota((128, 128), 1) <= place, 1.0, 0.0).astype(bf)
     low_block = lax.dot_general(under, rep, both, preferred_element_type=f32)
     top_block = lax.dot_general(upon, rep, both, preferred_element_type=f32)
-    first = lax.dot_general(
-        start[...], jnp.broadcast_to(few[0:1, :].astype(f32), (128, 256)).astype(bf), both, preferred_element_type=f32
-    )
-    for j in range(BLOCKS // 128):
+    for n in range(8):
+        tab[n : n + 1, 256:TAB] = jnp.broadcast_to(top_block[127:128, 0:1], (1, TAB - 256)).astype(jnp.int32)
+    lows = []
+    for r in range(11):
+        base_tile = jnp.zeros((8, 128), f32)
+        for s in range(8):
+            v = r * 8 + s
+            if v < 81:
+                c = v // 9
+                base_tile = jnp.where(row == s, float(((c // 3) * 4 + c % 3) * COLUMN + 7 + v % 9), base_tile)
+        lows.append(base_tile)
+    for j in range(TAB // 128):
         b = (lane + 128 * j).astype(f32)
-        begin = jnp.zeros((8, 128), f32)
         low = jnp.zeros((8, 128), f32)
         for r in range(11):
-            base_tile = jnp.zeros((8, 128), f32)
-            for s in range(8):
-                v = r * 8 + s
-                if v < 81:
-                    c = v // 9
-                    base_tile = jnp.where(
-                        row == s, float(((c // 3) * 4 + c % 3) * COLUMN + 7 + v % 9), base_tile
-                    )
-            lo = low_block[r * 8 : r * 8 + 8, :]
-            hit = (lo <= b) & (b < top_block[r * 8 : r * 8 + 8, :])
-            begin = begin + jnp.where(hit, first[r * 8 : r * 8 + 8, :] + 16.0 * (b - lo) - SPARE, 0.0)
-            low = low + jnp.where(hit, base_tile, 0.0)
-        tab[3:4, j * 128 : j * 128 + 128] = (jnp.sum(begin, axis=0, keepdims=True) + SPARE).astype(jnp.int32)
-        tab[4:5, j * 128 : j * 128 + 128] = jnp.sum(low, axis=0, keepdims=True).astype(jnp.int32)
-    tab[5:6, 0:128] = top_block[127:128, :].astype(jnp.int32)
+            lo, hi = low_block[r * 8 : r * 8 + 8, :], top_block[r * 8 : r * 8 + 8, :]
+            low = low + jnp.where((lo <= b) & (b < hi), lows[r], 0.0)
+        tab[7:8, j * 128 : j * 128 + 128] = jnp.sum(low, axis=0, keepdims=True).astype(jnp.int32)
     stores[4].start()
 
     for c in copies:
@@ -321,31 +337,32 @@
     return (tile // 16 + 1) * (4 * COLUMN) + (tile // 8 % 2 + 1) * COLUMN + tile % 8 + 8
 
 
-def pack_rows(tab, order, rows, packed):
+def pack_rows(tab, rows, packed):
+    part = lax.shift_right_logical(iota((8, 128), 1), 4)
+
     def step(i, carry):
-        items = [order[i * 8 + u] for u in range(8)]
-        widest = tab[2, items[0]]
-        for item in items[1:]:
-            widest = jnp.maximum(widest, tab[2, item])
+        widest = tab[6, i * 8]
+
+        def move(u, k):
+            code, dst = tab[3, i * 8 + u], tab[4, i * 8 + u]
+            src = lax.shift_right_logical(code, 3)
+            value = rows[pl.ds(src + 8 * k, 8), :]
+            packed[pl.ds(dst + 8 * k, 8), :] = jnp.where(part == (code & 7), value, 0.0)
 
         @pl.when(widest <= FAST * 8)
         def _():
-            for item in items:
-                src, dst = tab[1, item], tab[0, item]
+            for u in range(8):
                 for k in range(FAST):
-                    packed[pl.ds(dst + 8 * k, 8), :] = rows[pl.ds(src + 8 * k, 8), :]
+                    move(u, k)
 
         @pl.when(widest > FAST * 8)
         def _():
             def one(u, carry):
-                item = order[i * 8 + u]
-                src, dst = tab[1, item], tab[0, item]
-
                 def inner(k, carry):
-                    packed[pl.ds(dst + 8 * k, 8), :] = rows[pl.ds(src + 8 * k, 8), :]
+                    move(u, k)
                     return carry
 
-                return lax.fori_loop(0, (tab[2, item] + 7) // 8, inner, carry)
+                return lax.fori_loop(0, (tab[5, i * 8 + u] + 7) // 8, inner, carry)
 
             lax.fori_loop(0, 8, one, 0)
 
@@ -358,8 +375,6 @@
     def step(tile, carry):
         first = tile // 8 * 64 + tile % 8
         widest = tab[2, first]
-        for o in range(1, 8):
-            widest = jnp.maximum(widest, tab[2, first + o * 8])
 
         @pl.when(widest <= FAST * 8)
         def _():
@@ -377,7 +392,7 @@
                 def inner(k, lanes):
                     return chunk(item, tile, o, k, lanes)
 
-                return lax.fori_loop(0, (tab[2, item] + 7) // 8, inner, lanes)
+                return lax.fori_loop(0, (tab[1, item] + 7) // 8, inner, lanes)
 
             put(tile, lax.fori_loop(0, 8, per, zero))
 
@@ -404,29 +419,28 @@
 
 
 def density_kernel(
-    tab_h, order_h, jf_h, key_h, rows_h, w_h, ti_h, tl_h,
-    tab, order, jf, key, rows, packed, ti, tl, wb, own, last, insem, outsem, wsem,
+    tab_h, jf_h, key_h, rows_h, w_h, tl_h,
+    tab, jf, key, rows, packed, ti, tl, wb, own, last, insem, outsem, wsem,
 ):
     loads = [
         pltpu.make_async_copy(src, dst, insem.at[n])
-        for n, (src, dst) in enumerate(((tab_h, tab), (order_h, order), (rows_h, rows.at[0:4096]), (jf_h, jf), (key_h, key)))
+        for n, (src, dst) in enumerate(((tab_h, tab), (rows_h, rows.at[0:512]), (jf_h, jf), (key_h, key)))
     ]
     for c in loads:
         c.start()
-    for c in loads[:3]:
-        c.wait()
-    pack_rows(tab, order, rows, packed)
-    for c in loads[3:]:
-        c.wait()
-    count = tab[5, 0]
-    third = lax.rem(iota((8, 128), 1), 3)
-    masks = [(third == n) & (iota((8, 128), 1) < 9) for n in range(3)]
+    for c in loads[:2]:
+        c.wait()
+    pack_rows(tab, rows, packed)
+    for c in loads[2:]:
+        c.wait()
+    count = tab[0, 256]
+    feature = iota((8, 128), 1) & 15
+    masks = [(feature == n) | (feature == n + 3) | (feature == n + 6) for n in range(3)]
 
     def own_rows(b):
-        row = tab[3, b]
         out = []
-        for k in range(2):
-            value = packed[pl.ds(row + 8 * k, 8), :]
+        for k in range(PER):
+            value = packed[pl.ds(pl.multiple_of(b * BLOCK + 8 * k, 8), 8), :]
             x, y, z = (wide(jnp.sum(jnp.where(m, value, 0.0), axis=1, keepdims=True)) for m in masks)
             out += [x + x, y + y, z + z, 1.0 - (x * x + y * y + z * z)]
         return out
@@ -438,31 +452,33 @@
 
     def settle(i, tots):
         for u in range(STEP):
-            row = tab[3, i * STEP + u]
-            for k in range(2):
-                ti[pl.ds(row + 8 * k, 8), :] = slope_of(tots[u][k])
+            b = i * STEP + u
+            for k in range(PER):
+                t = slope_of(tots[u][k])
+                ti[pl.ds(pl.multiple_of(b * BLOCK + 8 * k, 8), 8), :] = t
+                wb[b, (8 * PER + k) * 8 : (8 * PER + k) * 8 + 8, :] = t
 
     def step(i, carry):
-        tots = [[last[u, k] for k in range(2)] for u in range(STEP)]
-        ahead = [own_rows((i + 1) * STEP + u) for u in range(STEP)]
+        tots = [[last[u, k] for k in range(PER)] for u in range(STEP)]
+        ahead = [own_rows(jnp.minimum((i + 1) * STEP + u, BLOCKS - 1)) for u in range(STEP)]
         new = []
         for u in range(STEP):
             b = i * STEP + u
-            mine = [[own[u, 4 * k + n] for n in range(4)] for k in range(2)]
-            tot = [None, None]
-            for n, tile in enumerate(around(tab[4, b])):
+            mine = [[own[u, 4 * k + n] for n in range(4)] for k in range(PER)]
+            tot = [None] * PER
+            for n, tile in enumerate(around(tab[7, b])):
                 xj, yj, zj, bj = (jf[m, pl.ds(tile, 8, stride=0), :] for m in range(4))
-                for k in range(2):
+                for k in range(PER):
                     x, y, z, a = mine[k]
                     w = jnp.maximum((a + bj) + (x * xj + y * yj + z * zj), 0.0)
-                    wb[b, (n * 2 + k) * 8 : (n * 2 + k) * 8 + 8, :] = w
+                    wb[b, (n * PER + k) * 8 : (n * PER + k) * 8 + 8, :] = w
                     cube = w * w * w
                     tot[k] = cube if tot[k] is None else tot[k] + cube
             new.append(tot)
         settle(jnp.maximum(i - 1, 0), tots)
         keep(ahead)
         for u in range(STEP):
-            for k in range(2):
+            for k in range(PER):
                 last[u, k] = new[u][k]
         return carry
 
@@ -476,15 +492,18 @@
 
     def group(g, carry):
         lax.fori_loop(g * per, jnp.minimum(g * per + per, steps), step, 0)
-        saved(g).start()
+
+        @pl.when(g > 0)
+        def _():
+            saved(g - 1).start()
+
         return carry
 
     keep([own_rows(u) for u in range(STEP)])
     last[...] = jnp.ones_like(last)
     lax.fori_loop(0, groups, group, 0)
-    settle(steps - 1, [[last[u, k] for k in range(2)] for u in range(STEP)])
-    rows_out = pltpu.make_async_copy(ti, ti_h, outsem.at[0])
-    rows_out.start()
+    settle(steps - 1, [[last[u, k] for k in range(PER)] for u in range(STEP)])
+    saved(groups - 1).start()
 
     match = matcher(key)
 
@@ -496,7 +515,7 @@
         tl[pl.ds(tile, 1), :] = jnp.sum(lanes, axis=0, keepdims=True)
 
     over_tiles(tab, finish, put, jnp.zeros((8, 128), f32))
-    lanes_out = pltpu.make_async_copy(tl, tl_h, outsem.at[1])
+    lanes_out = pltpu.make_async_copy(tl, tl_h, outsem.at[0])
     lanes_out.start()
 
     def drain(g, carry):
@@ -504,7 +523,6 @@
         return carry
 
     lax.fori_loop(0, groups, drain, 0)
-    rows_out.wait()
     lanes_out.wait()
 
 
@@ -530,8 +548,8 @@
 
 
 def force_kernel(
-    tab_h, w_h, jf_h, tj_h, key_h, ti_h, pv_h, heat_h, vel_h, temp,
-    tab, wb, jf, tj, key, ti, pv, heat, vel, fg, fx, fy, fz, last, old, new, insem, outsem, wsem,
+    tab_h, w_h, jf_h, tj_h, key_h, pv_h, heat_h, vel_h, temp_h,
+    tab, wb, jf, tj, key, pv, heat, vel, temp, fg, fx, fy, fz, last, old, new, insem, outsem, wsem,
 ):
     def loaded(g):
         part = pl.ds(g * CHUNK, CHUNK)
@@ -541,7 +559,7 @@
         pltpu.make_async_copy(src, dst, insem.at[n])
         for n, (src, dst) in enumerate(
             (
-                (tab_h, tab), (heat_h, heat), (tj_h, tj.at[:, 8:16]), (ti_h, ti),
+                (tab_h, tab), (heat_h, heat), (tj_h, tj.at[:, 8:16]),
                 (jf_h.at[0:3], jf), (key_h, key), (pv_h, pv),
             )
         )
@@ -551,7 +569,7 @@
     for c in loads[1:]:
         c.start()
     loads[0].wait()
-    count = tab[5, 0]
+    count = tab[0, 256]
     groups = (count + CHUNK - 1) // CHUNK
 
     def fetch(g, carry):
@@ -565,38 +583,39 @@
         tj[col, 16:24, :] = none
     loads[1].wait()
     diffuse(heat, temp, old, new)
+    warm = pltpu.make_async_copy(temp, temp_h, outsem.at[1])
+    warm.start()
     for c in loads[2:]:
         c.wait()
     sums = (fg, fx, fy, fz)
 
     def settle(i):
         for u in range(STEP):
-            row = tab[3, i * STEP + u]
-            for k in range(2):
+            row = (i * STEP + u) * BLOCK
+            for k in range(PER):
                 for n, f in enumerate(sums):
-                    f[pl.ds(row + 8 * k, 8), :] = wide(jnp.sum(last[u, 4 * k + n], axis=1, keepdims=True))
+                    at = pl.ds(pl.multiple_of(row + 8 * k, 8), 8)
+                    f[at, :] = wide(jnp.sum(last[u, 4 * k + n], axis=1, keepdims=True))
 
     def step(i, carry):
         settle(jnp.maximum(i - 1, 0))
         new = []
         for u in range(STEP):
             b = i * STEP + u
-            low = tab[4, b]
-            row = tab[3, b]
-            t_own = [ti[pl.ds(row + 8 * k, 8), :] for k in range(2)]
-            tot = [None] * 8
-            for n, tile in enumerate(around(low)):
+            t_own = [wb[b, (8 * PER + k) * 8 : (8 * PER + k) * 8 + 8, :] for k in range(PER)]
+            tot = [None] * (4 * PER)
+            for n, tile in enumerate(around(tab[7, b])):
                 other = [jf[m, pl.ds(tile, 8, stride=0), :] for m in range(3)]
                 t_other = tj.at[...].reshape(16 * COLUMN, 128)[pl.ds(tile, 8, stride=0), :]
-                for k in range(2):
-                    w = wb[b, (n * 2 + k) * 8 : (n * 2 + k) * 8 + 8, :]
+                for k in range(PER):
+                    w = wb[b, (n * PER + k) * 8 : (n * PER + k) * 8 + 8, :]
                     g = (w * w) * ((t_own[k] + t_other) - w)
                     for m, p in enumerate((g, g * other[0], g * other[1], g * other[2])):
                         at = 4 * k + m
                         tot[at] = p if tot[at] is None else tot[at] + p
             new.append(tot)
         for u in range(STEP):
-            for n in range(8):
+            for n in range(4 * PER):
                 last[u, n] = new[u][n]
         return carry
 
@@ -633,9 +652,9 @@
     out = pltpu.make_async_copy(vel, vel_h, outsem.at[0])
     out.start()
     out.wait()
-
-
-VMEM = pl.BlockSpec(memory_space=pltpu.VMEM)
+    warm.wait()
+
+
 ANY = pl.BlockSpec(memory_space=pltpu.HBM)
 LOCAL = pltpu.CompilerParams(vmem_limit_bytes=67043328)
 
@@ -653,7 +672,7 @@
 
 
 def local(positions, velocities, kicks, counts, subcell, electron_temp, laser_flux):
-    order, *zeroone = static_tables()
+    *zeroone, source = static_tables()
     upper = np.triu(np.ones((128, 128)))
     bf = jnp.bfloat16
     i32 = jnp.int32
@@ -663,10 +682,10 @@
     outs = (
         shape(4, 16 * COLUMN, 128),
         shape(TILES, 128, dtype=i32),
-        shape(8, BLOCKS, dtype=i32),
+        shape(8, TAB, dtype=i32),
         shape(2, 2, 3, 8, 128),
         shape(3, TILES, 128),
-        shape(4096, 128),
+        shape(512, 128),
     )
     jf, key, tab, heat, pv, rows = pl.pallas_call(
         gather_kernel,
@@ -682,6 +701,7 @@
             pltpu.SMEM((6, 6), f32),
             pltpu.VMEM((128, 128), bf),
             *(pltpu.VMEM(m.shape, bf) for m in zeroone),
+            pltpu.VMEM(source.shape, i32),
             *(vmem(o) for o in outs),
             pltpu.VMEM((3, 4, 4, 8, 128), f32),
             pltpu.VMEM((8, 2, 2, 8), i32),
@@ -695,34 +715,33 @@
         compiler_params=meeting(0),
     )(
         positions, velocities, kicks, counts, subcell, electron_temp, laser_flux,
-        *(jnp.asarray(m, bf) for m in (upper, *zeroone)),
+        *(jnp.asarray(m, bf) for m in (upper, *zeroone)), jnp.asarray(source),
     )
-    order = jnp.asarray(order)
     row = shape(ROWS, 128)
-    w, ti, tl = pl.pallas_call(
+    saved = shape(BLOCKS, WIDE, 128)
+    w, tl = pl.pallas_call(
         density_kernel,
         name="density",
-        out_shape=(shape(BLOCKS, 128, 128), row, shape(TILES, 128)),
-        in_specs=[ANY] * 5,
-        out_specs=(ANY,) * 3,
+        out_shape=(saved, shape(TILES, 128)),
+        in_specs=[ANY] * 4,
+        out_specs=(ANY,) * 2,
         scratch_shapes=[
-            pltpu.SMEM((8, BLOCKS), i32),
-            pltpu.SMEM((256,), i32),
+            pltpu.SMEM((8, TAB), i32),
             vmem(outs[0]),
             vmem(outs[1]),
-            vmem(row),
+            pltpu.VMEM((1024, 128), f32),
             vmem(row),
             vmem(row),
             pltpu.VMEM((TILES, 128), f32),
-            pltpu.VMEM((BLOCKS, 128, 128), f32),
-            pltpu.VMEM((STEP, 8, 8, 128), f32),
-            pltpu.VMEM((STEP, 2, 8, 128), f32),
-            dma((5,)),
-            dma((2,)),
+            vmem(saved),
+            pltpu.VMEM((STEP, 4 * PER, 8, 128), f32),
+            pltpu.VMEM((STEP, PER, 8, 128), f32),
+            dma((4,)),
+            dma((1,)),
             dma((BLOCKS // CHUNK,)),
         ],
         compiler_params=LOCAL,
-    )(tab, order, jf, key, rows)
+    )(tab, jf, key, rows)
     t_all, heat = pl.pallas_call(
         exchange_kernel,
         name="exchange",
@@ -736,27 +755,27 @@
         force_kernel,
         name="force",
         out_shape=(shape(3, TILES, 128), shape(6, 6, 24)),
-        in_specs=[ANY] * 8,
-        out_specs=(ANY, VMEM),
+        in_specs=[ANY] * 7,
+        out_specs=(ANY,) * 2,
         scratch_shapes=[
-            pltpu.SMEM((8, BLOCKS), i32),
-            pltpu.VMEM((BLOCKS, 128, 128), f32),
+            pltpu.SMEM((8, TAB), i32),
+            vmem(saved),
             pltpu.VMEM((3, 16 * COLUMN, 128), f32),
             pltpu.VMEM((16, COLUMN, 128), f32),
             vmem(outs[1]),
-            vmem(row),
             vmem(outs[4]),
             pltpu.VMEM((4, 4, 3, 8, 128), f32),
             vmem(outs[4]),
+            pltpu.VMEM((6, 6, 24), f32),
             *(vmem(row),) * 4,
-            pltpu.VMEM((STEP, 8, 8, 128), f32),
+            pltpu.VMEM((STEP, 4 * PER, 8, 128), f32),
             *(pltpu.VMEM((12, 24, 128), f32),) * 2,
-            dma((7,)),
-            dma((1,)),
+            dma((6,)),
+            dma((2,)),
             dma((BLOCKS // CHUNK,)),
         ],
         compiler_params=LOCAL,
-    )(tab, w, jf, t_all.reshape(16, 8, 128), key, ti, pv, heat)
+    )(tab, w, jf, t_all.reshape(16, 8, 128), key, pv, heat)
     return (vel.reshape(3, 2, 2, 8, 128), temp)
 
 

time: 57.7 us -> 54.8 us (0.950)
  the two profiles are of different devices: /device:TPU:1 before, /device:TPU:0 now
where the time goes in v1:
time: 54.8 us; the launch traced here: 54.5 us
  Pallas kernels  53.9 us (98%)
  between operations  0.66 us (1%)
    pallas_call x1, Pallas kernels, local(): pl.pallas_call(density_kernel, name='density', out_shape=(saved, shape(TI...  16.8 us
    pallas_call x1, Pallas kernels, local(): pl.pallas_call(gather_kernel, name='gather', out_shape=outs, in_specs=[AN...  13 us
    pallas_call x1, Pallas kernels, local(): pl.pallas_call(force_kernel, name='force', out_shape=(shape(3, TILES, 128...  12.7 us
    pallas_call x1, Pallas kernels, local(): pl.pallas_call(exchange_kernel, name='exchange', out_shape=(shape(4, 4, 8...  11.4 us

profile of v1, /device:TPU:0, one launch (start us, length us, event | category | flops | bytes accessed | tf_op | source)
XLA Modules:
  0.0 54.5 jit_solution(17470268395913991083)
XLA Ops:
  0.6 13.0 %gather.1 = (f32[4,384,128]{2,1,0:T(8,128)}, s32[32,128]{1,0:T(8,128)}, s32[8,640]{1,0:T(8,128)}, f32[2,2,3,8,128]{4,3,2,1,0:T(8,128)}, f32[3,32,128]{2,1,0:T(8,128)}, /*index=5*/f32[512,128]{1,0:T(8,128)}) custom-call(f32[3,2,2,8,128]{4,3,2,1,0:T(8,128)} %pos_h.1, f32[3,2,2,8,128]{4,3,2,1,0:T(8,128)} %vel_h.1, f32[3,2,2,8,128]{4,3,2,1,0:T(8,128)} %kick_h.1, ...), custom_call_target="tpu_custom_call" | custom-call | tf_op jit(solution)/shard_map/gather/pallas_call | solution.py:690
  13.6 16.8 %density.1 = (f32[608,72,128]{2,1,0:T(8,128)}, f32[32,128]{1,0:T(8,128)}) custom-call(s32[8,640]{1,0:T(8,128)} %get-tuple-element.14.tab_h, f32[4,384,128]{2,1,0:T(8,128)} %get-tuple-element.15.jf_h, s32[32,128]{1,0:T(8,128)} %get-tuple-element.16.key_h, f32[512,128]{1,0:T(8,128)} %get-tuple-element.17.rows_h), custom_call_target="tpu_custom_call" | custom-call | tf_op jit(solution)/shard_map/density/pallas_call | solution.py:722
  30.4 11.4 %exchange.1 = (f32[4,4,8,128]{3,2,1,0:T(8,128)}, f32[4,4,3,8,128]{4,3,2,1,0:T(8,128)}) custom-call(f32[2,2,8,128]{3,2,1,0:T(8,128)} %bitcast.4, f32[2,2,3,8,128]{4,3,2,1,0:T(8,128)} %get-tuple-element.20.heat), custom_call_target="tpu_custom_call" | custom-call | tf_op jit(solution)/shard_map/exchange/pallas_call | solution.py:745
  41.9 12.7 %force.1 = (f32[3,32,128]{2,1,0:T(8,128)}, f32[6,6,24]{2,1,0:T(8,128)}) custom-call(s32[8,640]{1,0:T(8,128)} %get-tuple-element.14.tab_h, f32[608,72,128]{2,1,0:T(8,128)} %get-tuple-element.18.w_h, f32[4,384,128]{2,1,0:T(8,128)} %get-tuple-element.15.jf_h, f32[16,8,128]{2,1,0:T(8,128)} %bitcast.3, s32[32,128]{1,0:T(8,128)} %get-tuple-element.16.key_h, ...), custom_call_target="tpu_custom_call" | custom-call | tf_op jit(solution)/shard_map/force/pallas_call | solution.py:754
